TPU v7x, 32 devices: a whole 2x2x4 slice. The times are simulated.
32 devices in a mesh: dom: 8 (over z, y), cluster: 4 (over x, core).
Axes of the slice: x: 2, y: 2, z: 4, core: 2. Of those that a mesh axis runs over, the one named last changes fastest.
Arguments:
- features: bfloat16 [4, 6144, 512], P('cluster', 'dom'), may hold values from -6 to 6
- stale: bfloat16 [4, 256, 512], P('cluster'), may hold values from -6 to 6
- boundary: int32 [4, 8], P('cluster', 'dom'), may hold values from 0 to 23
- skip: int32 [4, 8], P('cluster'), may hold values 0 or 1
- tile_vals: bfloat16 [4, 256, 32, 128], P('cluster', 'dom'), may hold values from -0.4375 to 0.4375
- tile_row: int32 [4, 256], P('cluster', 'dom'), may hold values from 0 to 5
- tile_src: int32 [4, 256], P('cluster', 'dom'), may hold values from 0 to 9
- tile_count: int32 [4, 8], P('cluster', 'dom'), may hold values from 16 to 32, as said below
- weight: bfloat16 [512, 512], replicated, may hold values from -0.25 to 0.25
- cotangent: bfloat16 [4, 6144, 512], P('cluster', 'dom'), may hold values from -6 to 6
Outputs:
- out_features: bfloat16 [4, 6144, 512], P('cluster', 'dom')
- grad_features: bfloat16 [4, 6144, 512], P('cluster', 'dom')
- grad_weight: float32 [512, 512], P('dom')
Inputs may be any that keep to these rules, and one draw needn't show every extreme that they name: `tile_count`: every partition has at least half of its slots live; some partition has all 32 slots live.
All inputs are finite; a program needn't handle non-finite values. No bound on the sum of `skip` on one device may be relied on, other than what follows from the above.
Results may differ from a plain program's by a relative error of at most 0.02.
Values may be sent and summed in bfloat16 or wider, within the bound.
A program may use at most 64 MiB of HBM per device.

v0:
```python
import jax
import jax.numpy as jnp
from jax import lax
from jax.sharding import PartitionSpec as P


def padded(cells, sides, width):
    for axis, dim in sides:
        count = lax.axis_size(axis)
        head = lax.slice_in_dim(cells, 0, width, axis=dim)
        tail = lax.slice_in_dim(cells, cells.shape[dim] - width, cells.shape[dim], axis=dim)
        cells = jnp.concatenate(
            [
                lax.ppermute(tail, axis, [(i, (i + 1) % count) for i in range(count)]),
                cells,
                lax.ppermute(head, axis, [((i + 1) % count, i) for i in range(count)]),
            ],
            axis=dim,
        )
    return cells


def passed_along(x, axis, by):
    count = lax.axis_size(axis)
    return lax.ppermute(x, axis, [(i, (i + by) % count) for i in range(count)])


def silu_parts(value):
    sig = jax.nn.sigmoid(value)
    return (value * sig, sig * (1.0 + value * (1.0 - sig)))


def per_device(
    features, stale, boundary, skip, tile_vals, tile_row, tile_src, tile_count, weight, cotangent
):
    feats = features[0]
    nodes, width = feats.shape
    parts = lax.axis_size("dom")
    blk = stale.shape[1] // parts
    tile_blocks = tile_vals[0]
    slots, _, tile_rows = tile_blocks.shape
    row_blocks = nodes // tile_rows
    start_row = boundary[0, 0] * blk
    own_block = lax.dynamic_slice_in_dim(feats, start_row, blk, 0)
    gathered = lax.all_gather(own_block, "dom", axis=0, tiled=True).reshape(parts, blk, width)
    beside_all = padded(own_block[None], (("cluster", 0),), 1)
    skipped = skip[0] == 1
    fresh = jnp.where(skipped[:, None, None], stale[0].reshape(parts, blk, width), gathered)
    table = jnp.concatenate([fresh, beside_all[0:1], beside_all[2:3]], axis=0)
    active_mask = (jnp.arange(slots, dtype=jnp.int32) < tile_count[0, 0]).astype(jnp.float32)
    sources = tile_src[0]
    targets = tile_row[0]
    selected_block = jnp.take(table, sources, axis=0)
    contribution = (
        jnp.einsum("wnz,wnx->wzx", tile_blocks, selected_block, preferred_element_type=jnp.float32)
        * active_mask[:, None, None]
    )
    row_onehot_mask = (targets[:, None] == jnp.arange(row_blocks, dtype=jnp.int32)[None, :]).astype(
        jnp.float32
    )
    row_onehot_mask = row_onehot_mask * active_mask[:, None]
    aggregate_block_list = jnp.einsum(
        "xn,xij->nij", row_onehot_mask, contribution, precision=lax.Precision.HIGHEST
    )
    agg = (feats.astype(jnp.float32) + aggregate_block_list.reshape(nodes, width)).astype(
        jnp.bfloat16
    )
    zval = jnp.dot(agg, weight, preferred_element_type=jnp.float32)
    act, slope = silu_parts(zval)
    out_features = act.astype(jnp.bfloat16)
    dz = (cotangent[0].astype(jnp.float32) * slope).astype(jnp.bfloat16)
    dagg = lax.dot_general(
        dz, weight, (((1,), (1,)), ((), ())), preferred_element_type=jnp.float32
    ).astype(jnp.bfloat16)
    selected_rows = jnp.take(dagg.reshape(row_blocks, tile_rows, width), targets, axis=0)
    selected_gradient = (
        jnp.einsum("dck,dkn->dcn", tile_blocks, selected_rows, preferred_element_type=jnp.float32)
        * active_mask[:, None, None]
    )
    src_hot = (sources[:, None] == jnp.arange(parts + 2, dtype=jnp.int32)[None, :]).astype(
        jnp.float32
    )
    dsrc = jnp.einsum("ts,tbf->sbf", src_hot, selected_gradient, precision=lax.Precision.HIGHEST)
    keep = 1.0 - skipped.astype(jnp.float32)
    in_group = dsrc[:parts] * keep[:, None, None]
    from_upper = passed_along(dsrc[parts].astype(jnp.bfloat16), "cluster", -1).astype(jnp.float32)
    from_lower = passed_along(dsrc[parts + 1].astype(jnp.bfloat16), "cluster", 1).astype(
        jnp.float32
    )
    share = width // parts
    term_all = lax.dot_general(
        agg, dz, (((0,), (0,)), ((), ())), preferred_element_type=jnp.float32
    ).reshape(parts, share, width)
    stacked = jnp.concatenate([in_group, term_all], axis=1).reshape(parts * (blk + share), width)
    summed = lax.psum_scatter(
        stacked.astype(jnp.bfloat16), "dom", scatter_dimension=0, tiled=True
    ).astype(jnp.float32)
    mine = summed[:blk]
    grad_weight = lax.psum(summed[blk:].astype(jnp.bfloat16), "cluster").astype(jnp.float32)
    bgrad = mine + from_upper + from_lower
    full = dagg.astype(jnp.float32)
    current = lax.dynamic_slice_in_dim(full, start_row, blk, 0)
    full = lax.dynamic_update_slice_in_dim(full, current + bgrad, start_row, 0)
    grad_features = full.astype(jnp.bfloat16)
    return (out_features[None], grad_features[None], grad_weight)


def solution(mesh):
    return jax.shard_map(
        per_device,
        mesh=mesh,
        in_specs=(
            P("cluster", "dom", None),
            P("cluster", None, None),
            P("cluster", "dom"),
            P("cluster", None),
            P("cluster", "dom", None, None),
            P("cluster", "dom"),
            P("cluster", "dom"),
            P("cluster", "dom"),
            P(),
            P("cluster", "dom", None),
        ),
        out_specs=(P("cluster", "dom", None), P("cluster", "dom", None), P("dom", None)),
        check_vma=False,
    )
```

profile of v0, /device:TPU:0, one launch (start us, length us, event | category | flops | bytes accessed | tf_op | source)
XLA Modules:
  0.0 193.5 jit_solution(16718258283287903912)
XLA Ops:
  8.0 0.8 constant_dynamic-slice_fusion
  8.7 0.5 collective-permute-start
  9.2 1.9 collective-permute-start.1
  11.1 31.9 %all-gather = bf16[1,256,512]{2,1,0:T(8,128)(2,1)S(1)} all-gather(bf16[1,32,512]{2,1,0:T(8,128)(2,1)S(1)} %constant_dynamic-slice_fusion), channel_id=2, replica_groups=mesh['dom'=8,'cluster'=4] {'dom'}, dimensions={1}, use_global_device_ids=true | all-gather | bytes 294912 | tf_op jit(solution)/shard_map/all_gather | solution.py:45
  43.0 0.7 fusion.30
  43.7 0.7 compare_and_fusion.1
  44.3 0.7 fusion.31
  45.0 0.7 compare_and_fusion
  45.7 0.7 compare_bitcast_fusion
  46.3 0.7 convert_subtract_fusion
  47.7 1.1 broadcast_select_fusion
  48.8 0.6 gather_fusion
  49.4 4.6 %fusion.13 = f32[32,512,128]{2,1,0:T(8,128)} fusion(bf16[32,32,512]{2,1,0:T(8,128)(2,1)S(1)} %gather_fusion, pred[32]{0:T(512)(128)(4,1)S(1)} %compare_and_fusion.1, bf16[1,32,32,128]{3,2,1,0:T(8,128)(2,1)S(1)} %copy-done.1), kind=kOutput, calls=%fused_computation.22 | convolution fusion | flops 134742016 | bytes 9699360 | tf_op jit(solution)/shard_map/wnz,wnx->wzx/dot_general | solution.py:55
  54.1 10.3 %copy.20 = f32[32,512,128]{1,0,2:T(8,128)} copy(f32[32,512,128]{2,1,0:T(8,128)} %fusion.13) | data formatting | bytes 16777216 | tf_op jit(solution)/shard_map/wnz,wnx->wzx/dot_general | solution.py:55
  64.4 6.8 %fusion = f32[6,128,512]{2,0,1:T(8,128)S(1)} fusion(f32[32,512,128]{1,0,2:T(8,128)} %copy.20, f32[32]{0:T(128)S(1)} %compare_convert_fusion, s32[32]{0:T(128)S(1)} %bitcast.72), kind=kOutput, calls=%fused_computation.2 | convolution fusion | flops 153092480 | bytes 9961728 | tf_op jit(solution)/shard_map/xn,xij->nij/dot_general | solution.py:62
  71.2 0.9 copy.16
  72.6 1.2 copy.17
  73.8 2.0 %fusion.10 = (bf16[768,512]{1,0:T(8,128)(2,1)S(1)}, bf16[1,768,512]{2,1,0:T(8,128)(2,1)}) fusion(bf16[1,768,512]{2,1,0:T(8,128)(2,1)S(1)} %copy-done.7, bf16[768,512]{1,0:T(8,128)(2,1)S(1)} %fusion.11, bf16[512,512]{1,0:T(8,128)(2,1)S(1)} %copy-done), kind=kOutput, calls=%fused_computation.14 | convolution fusion | flops 407371776 | bytes 3670016 | tf_op jit(solution)/shard_map/dot_general | solution.py:68
  75.8 0.6 fusion.35
  76.4 0.5 copy-done.3
  76.9 1.4 convolution_convert_fusion.1
  78.3 2.8 %gather_fusion.1 = bf16[32,128,512]{2,1,0:T(8,128)(2,1)} fusion(bf16[6,128,512]{2,1,0:T(8,128)(2,1)S(1)} %bitcast.66, s32[1024]{0:T(1024)S(1)} %pad_clamp_fusion), kind=kCustom, calls=%fused_computation.1 | custom fusion | bytes 8388736 | tf_op jit(solution)/shard_map/jit(_take)/gather | solution.py:75
  81.0 3.1 %fusion.3 = f32[32,512,32]{1,2,0:T(8,128)S(1)} fusion(bf16[32,128,512]{2,1,0:T(8,128)(2,1)} %gather_fusion.1, pred[32]{0:T(512)(128)(4,1)S(1)} %compare_and_fusion, bf16[1,32,32,128]{3,2,1,0:T(8,128)(2,1)S(1)} %copy-done.1), kind=kOutput, calls=%fused_computation.5 | convolution fusion | flops 136314880 | bytes 6553632 | tf_op jit(solution)/shard_map/dck,dkn->dcn/dot_general | solution.py:77
  84.2 2.0 %fusion.7 = f32[10,32,512]{2,0,1:T(8,128)S(1)} fusion(f32[32,512,32]{1,2,0:T(8,128)S(1)} %fusion.3, f32[32]{0:T(128)S(1)} %compare_convert_fusion, s32[32]{0:T(128)S(1)} %bitcast.73), kind=kOutput, calls=%fused_computation.9 | convolution fusion | flops 63439168 | bytes 2752768 | tf_op jit(solution)/shard_map/ts,tbf->sbf/dot_general | solution.py:83
  86.4 1.0 pad_maximum_fusion
  87.9 0.5 collective-permute-start.3
  88.4 63.3 %reduce-scatter.2.cloned.1.call-done = bf16[96,512]{1,0:T(8,128)(2,1)} async-done(((bf16[768,512]{1,0:T(8,128)(2,1)}), bf16[96,512]{1,0:T(8,128)(2,1)}) %reduce-scatter.2.cloned.1.call-update) | async-done | bytes 98320 | tf_op jit(solution)/shard_map/reduce_scatter | solution.py:95
  151.7 1.5 slice.35
  153.2 0.8 add_dynamic-update-slice_fusion
  154.0 1.0 convert_bitcast_fusion
  155.0 30.2 %all-reduce.2.cloned.1.call-done = bf16[64,512]{1,0:T(8,128)(2,1)} async-done(((bf16[64,512]{1,0:T(8,128)(2,1)}), bf16[64,512]{1,0:T(8,128)(2,1)}) %all-reduce.2.cloned.1.call-update) | async-done | bytes 65552 | tf_op jit(solution)/shard_map/psum | solution.py:99
  185.2 1.5 convert_element_type.90
  (33 shorter events, 1.3 us)
Async XLA Ops:
  7.2 66.6 %copy-start = (bf16[512,512]{1,0:T(8,128)(2,1)S(1)}, bf16[512,512]{1,0:T(8,128)(2,1)}, u32[]{:S(2)}) copy-start(bf16[512,512]{1,0:T(8,128)(2,1)} %param.18) | copy-start | bytes 1572868
  7.2 42.2 %copy-start.1 = (bf16[1,32,32,128]{3,2,1,0:T(8,128)(2,1)S(1)}, bf16[1,32,32,128]{3,2,1,0:T(8,128)(2,1)}, u32[]{:S(2)}) copy-start(bf16[1,32,32,128]{3,2,1,0:T(8,128)(2,1)} %param.14) | copy-start | bytes 786436
  7.2 144.5 %reduce-scatter.2.cloned.1.call-start = ((), (), s32[]{:S(2)}) async-start(), calls=%async_computation.1 | async-start | bytes 884736 | tf_op jit(solution)/shard_map/reduce_scatter | solution.py:95
  8.7 40.0 %collective-permute-start = (bf16[1,32,512]{2,1,0:T(8,128)(2,1)S(1)}, bf16[1,32,512]{2,1,0:T(8,128)(2,1)S(1)}, u32[]{:S(2)}, u32[]{:S(2)}) collective-permute-start(bf16[1,32,512]{2,1,0:T(8,128)(2,1)S(1)} %constant_dynamic-slice_fusion), channel_id=1, source_target_pairs={{0,1},{1,2},{2,3},{3,0},{4,5},{5,6},{6,7},{7,4},{8,9},{9,10},{10,1... | collective-permute-start | bytes 98312 | tf_op jit(solution)/shard_map/ppermute | solution.py:14
  9.2 39.5 %collective-permute-start.1 = (bf16[1,32,512]{2,1,0:T(8,128)(2,1)S(1)}, bf16[1,32,512]{2,1,0:T(8,128)(2,1)S(1)}, u32[]{:S(2)}, u32[]{:S(2)}) collective-permute-start(bf16[1,32,512]{2,1,0:T(8,128)(2,1)S(1)} %constant_dynamic-slice_fusion), channel_id=1, source_target_pairs={{1,0},{2,1},{3,2},{0,3},{5,4},{6,5},{7,6},{4,7},{9,8},{10,9},{11,1... | collective-permute-start | bytes 98312 | tf_op jit(solution)/shard_map/ppermute | solution.py:16
  54.0 10.3 %copy-start.5 = (s32[1,32]{1,0:T(1,128)S(1)}, s32[1,32]{1,0:T(1,128)}, u32[]{:S(2)}) copy-start(s32[1,32]{1,0:T(1,128)} %param.15) | copy-start | bytes 388
  71.2 1.1 copy-start.2
  72.3 1.5 copy-start.7
  75.8 1.1 copy-start.3
  81.0 3.1 %copy-start.6 = (s32[1,32]{1,0:T(1,128)S(1)}, s32[1,32]{1,0:T(1,128)}, u32[]{:S(2)}) copy-start(s32[1,32]{1,0:T(1,128)} %param.16) | copy-start | bytes 388
  84.2 2.2 %copy-start.4 = (bf16[8,64,512]{2,1,0:T(8,128)(2,1)S(1)}, bf16[8,64,512]{2,1,0:T(8,128)(2,1)}, u32[]{:S(2)}) copy-start(bf16[8,64,512]{2,1,0:T(8,128)(2,1)} %convolution_convert_fusion.1) | copy-start | bytes 1572868
  87.4 97.8 %all-reduce.2.cloned.1.call-start = ((), (), s32[]{:S(2)}) async-start(), calls=%async_computation.2 | async-start | bytes 131072 | tf_op jit(solution)/shard_map/psum | solution.py:99
  87.8 65.4 %collective-permute-start.2 = (bf16[32,512]{1,0:T(8,128)(2,1)S(1)}, bf16[32,512]{1,0:T(8,128)(2,1)S(1)}, u32[]{:S(2)}, u32[]{:S(2)}) collective-permute-start(bf16[32,512]{1,0:T(8,128)(2,1)S(1)} %get-tuple-element.5), channel_id=1, source_target_pairs={{0,3},{1,0},{2,1},{3,2},{4,7},{5,4},{6,5},{7,6},{8,11},{9,8},{10,9... | collective-permute-start | bytes 98312 | tf_op jit(solution)/shard_map/ppermute | solution.py:25
  87.9 65.3 %collective-permute-start.3 = (bf16[32,512]{1,0:T(8,128)(2,1)S(1)}, bf16[32,512]{1,0:T(8,128)(2,1)S(1)}, u32[]{:S(2)}, u32[]{:S(2)}) collective-permute-start(bf16[32,512]{1,0:T(8,128)(2,1)S(1)} %get-tuple-element.6), channel_id=1, source_target_pairs={{0,1},{1,2},{2,3},{3,0},{4,5},{5,6},{6,7},{7,4},{8,9},{9,10},{10,1... | collective-permute-start | bytes 98312 | tf_op jit(solution)/shard_map/ppermute | solution.py:25
Sparse Core Ops, SparseCore 0:
  87.5 64.1 reduce-scatter.1
  154.6 30.5 all-reduce.1
where the time goes:
time: 194 us
  waiting for transfers between devices  93.6 us (48%)
  blocking collectives  31.9 us (16%)
  matrix products  20.5 us (11%)
  local copies, waits for them, and re-layouts  19.2 us (10%)
  between operations  15.6 us (8%)
  other arithmetic  9.72 us (5%)
  starting transfers between devices  3.04 us (2%)
    reduce_scatter x1, waiting for transfers between devices, per_device(): lax.psum_scatter(stacked.astype(jnp.bfloat16), 'dom', scatter_dimension=0...  63.3 us
    all_gather x1, blocking collectives, per_device(): lax.all_gather(own_block, 'dom', axis=0, tiled=True)  31.9 us
    psum x1, waiting for transfers between devices, per_device(): lax.psum(summed[blk:].astype(jnp.bfloat16), 'cluster').astype(jnp.float32)  30.2 us
    dot_general x1, local copies, waits for them, and re-layouts, per_device(): jnp.einsum('wnz,wnx->wzx', tile_blocks, selected_block, preferred_element...  10.3 us
    dot_general x1, matrix products, per_device(): jnp.einsum('xn,xij->nij', row_onehot_mask, contribution, precision=lax.Pr...  6.78 us
    dot_general x1, matrix products, per_device(): jnp.einsum('wnz,wnx->wzx', tile_blocks, selected_block, preferred_element...  4.61 us
  transfers between devices with their start and end apart: 6, of which 2 were waited for; matrix products, arithmetic and copies ran while one was open for 4% of the time, Pallas kernels for 0%

commit v1 on v0

--- a/solution.py
+++ b/solution.py
@@ -96,7 +96,9 @@
         stacked.astype(jnp.bfloat16), "dom", scatter_dimension=0, tiled=True
     ).astype(jnp.float32)
     mine = summed[:blk]
-    grad_weight = lax.psum(summed[blk:].astype(jnp.bfloat16), "cluster").astype(jnp.float32)
+    grad_weight = jnp.sum(
+        jax.lax.all_gather(summed[blk:].astype(jnp.bfloat16), axis_name="cluster"), axis=0
+    ).astype(jnp.float32)
     bgrad = mine + from_upper + from_lower
     full = dagg.astype(jnp.float32)
     current = lax.dynamic_slice_in_dim(full, start_row, blk, 0)

time: 194 us -> 167 us (0.86)
  waiting for transfers between devices: 93.6 us -> 63.4 us
  blocking collectives: 31.9 us -> 37.6 us
    psum x1 -> x0, waiting for transfers between devices: 30.2 us -> none  [per_device(): lax.psum(summed[blk:].astype(jnp.bfloat16), 'cluster').astype(jnp.float32)]
    all_gather x0 -> x1, blocking collectives: none -> 5.76 us  [per_device(): jax.lax.all_gather(summed[blk:].astype(jnp.bfloat16), axis_name='cluster')]
    ppermute x2, waiting for transfers between devices: 0.01 us -> 3.22 us  [passed_along(): return lax.ppermute(x, axis, [(i, (i + by) % count) for i in range(count)])]
    reduce_scatter x1, waiting for transfers between devices: 63.3 us -> 60.2 us  [per_device(): lax.psum_scatter(stacked.astype(jnp.bfloat16), 'dom', scatter_dimension=0...]
  transfers between devices with their start and end apart: 6 -> 5, of which waited for: 2 -> 3; matrix products, arithmetic and copies ran while one was open for 4% -> 3% of each run, Pallas kernels for 0% -> 0%
where the time goes in v1:
time: 167 us
  waiting for transfers between devices  63.4 us (38%)
  blocking collectives  37.6 us (23%)
  matrix products  20.5 us (12%)
  local copies, waits for them, and re-layouts  17.7 us (11%)
  between operations  15.6 us (9%)
  other arithmetic  8.95 us (5%)
  starting transfers between devices  3 us (2%)
    reduce_scatter x1, waiting for transfers between devices, per_device(): lax.psum_scatter(stacked.astype(jnp.bfloat16), 'dom', scatter_dimension=0...  60.2 us
    all_gather x1, blocking collectives, per_device(): lax.all_gather(own_block, 'dom', axis=0, tiled=True)  31.9 us
    dot_general x1, local copies, waits for them, and re-layouts, per_device(): jnp.einsum('wnz,wnx->wzx', tile_blocks, selected_block, preferred_element...  10.3 us
    dot_general x1, matrix products, per_device(): jnp.einsum('xn,xij->nij', row_onehot_mask, contribution, precision=lax.Pr...  6.78 us
    all_gather x1, blocking collectives, per_device(): jax.lax.all_gather(summed[blk:].astype(jnp.bfloat16), axis_name='cluster')  5.76 us
    dot_general x1, matrix products, per_device(): jnp.einsum('wnz,wnx->wzx', tile_blocks, selected_block, preferred_element...  4.62 us
  transfers between devices with their start and end apart: 5, of which 3 were waited for; matrix products, arithmetic and copies ran while one was open for 3% of the time, Pallas kernels for 0%

profile of v1, /device:TPU:0, one launch (start us, length us, event | category | flops | bytes accessed | tf_op | source)
XLA Modules:
  0.0 166.8 jit_solution(3950901149765136928)
XLA Ops:
  8.0 0.8 constant_dynamic-slice_fusion
  9.2 1.9 %collective-permute-start.1 = (bf16[1,32,512]{2,1,0:T(8,128)(2,1)S(1)}, bf16[1,32,512]{2,1,0:T(8,128)(2,1)S(1)}, u32[]{:S(2)}, u32[]{:S(2)}) collective-permute-start(bf16[1,32,512]{2,1,0:T(8,128)(2,1)S(1)} %constant_dynamic-slice_fusion), channel_id=1, source_target_pairs={{1,0},{2,1},{3,2},{0,3},{5,4},{6,5},{7,6},{4,7},{9,8},{10,9},{11,1... | collective-permute-start | bytes 98312 | tf_op jit(solution)/shard_map/ppermute | solution.py:16
  11.1 31.9 %all-gather = bf16[1,256,512]{2,1,0:T(8,128)(2,1)S(1)} all-gather(bf16[1,32,512]{2,1,0:T(8,128)(2,1)S(1)} %constant_dynamic-slice_fusion), channel_id=2, replica_groups=mesh['dom'=8,'cluster'=4] {'dom'}, dimensions={1}, use_global_device_ids=true | all-gather | bytes 294912 | tf_op jit(solution)/shard_map/all_gather | solution.py:45
  43.0 0.7 fusion.30
  43.7 0.7 compare_and_fusion.1
  44.3 0.7 fusion.31
  45.0 0.7 compare_and_fusion
  45.7 0.7 compare_bitcast_fusion
  46.3 0.7 convert_subtract_fusion
  47.7 1.1 broadcast_select_fusion
  48.8 0.6 gather_fusion
  49.4 4.6 %fusion.13 = f32[32,512,128]{2,1,0:T(8,128)} fusion(bf16[32,32,512]{2,1,0:T(8,128)(2,1)S(1)} %gather_fusion, pred[32]{0:T(512)(128)(4,1)S(1)} %compare_and_fusion.1, bf16[1,32,32,128]{3,2,1,0:T(8,128)(2,1)S(1)} %copy-done.1), kind=kOutput, calls=%fused_computation.22 | convolution fusion | flops 134742016 | bytes 9699360 | tf_op jit(solution)/shard_map/wnz,wnx->wzx/dot_general | solution.py:55
  54.1 10.3 %copy.20 = f32[32,512,128]{1,0,2:T(8,128)} copy(f32[32,512,128]{2,1,0:T(8,128)} %fusion.13) | data formatting | bytes 16777216 | tf_op jit(solution)/shard_map/wnz,wnx->wzx/dot_general | solution.py:55
  64.4 6.8 %fusion = f32[6,128,512]{2,0,1:T(8,128)S(1)} fusion(f32[32,512,128]{1,0,2:T(8,128)} %copy.20, f32[32]{0:T(128)S(1)} %compare_convert_fusion, s32[32]{0:T(128)S(1)} %bitcast.74), kind=kOutput, calls=%fused_computation.2 | convolution fusion | flops 153092480 | bytes 9961728 | tf_op jit(solution)/shard_map/xn,xij->nij/dot_general | solution.py:62
  71.2 0.9 copy.16
  72.6 1.2 copy.17
  73.8 2.0 %fusion.10 = (bf16[768,512]{1,0:T(8,128)(2,1)S(1)}, bf16[1,768,512]{2,1,0:T(8,128)(2,1)}) fusion(bf16[1,768,512]{2,1,0:T(8,128)(2,1)S(1)} %copy-done.7, bf16[768,512]{1,0:T(8,128)(2,1)S(1)} %fusion.11, bf16[512,512]{1,0:T(8,128)(2,1)S(1)} %copy-done), kind=kOutput, calls=%fused_computation.14 | convolution fusion | flops 407371776 | bytes 3670016 | tf_op jit(solution)/shard_map/dot_general | solution.py:68
  75.7 0.6 fusion.35
  76.4 0.5 copy-done.3
  76.9 1.4 convolution_convert_fusion.1
  78.2 2.8 %gather_fusion.1 = bf16[32,128,512]{2,1,0:T(8,128)(2,1)} fusion(bf16[6,128,512]{2,1,0:T(8,128)(2,1)S(1)} %bitcast.67, s32[1024]{0:T(1024)S(1)} %pad_clamp_fusion), kind=kCustom, calls=%fused_computation.1 | custom fusion | bytes 8388736 | tf_op jit(solution)/shard_map/jit(_take)/gather | solution.py:75
  81.0 3.1 %fusion.3 = f32[32,512,32]{1,2,0:T(8,128)S(1)} fusion(bf16[32,128,512]{2,1,0:T(8,128)(2,1)} %gather_fusion.1, pred[32]{0:T(512)(128)(4,1)S(1)} %compare_and_fusion, bf16[1,32,32,128]{3,2,1,0:T(8,128)(2,1)S(1)} %copy-done.1), kind=kOutput, calls=%fused_computation.5 | convolution fusion | flops 136314880 | bytes 6553632 | tf_op jit(solution)/shard_map/dck,dkn->dcn/dot_general | solution.py:77
  84.1 2.0 %fusion.7 = f32[10,32,512]{2,0,1:T(8,128)S(1)} fusion(f32[32,512,32]{1,2,0:T(8,128)S(1)} %fusion.3, f32[32]{0:T(128)S(1)} %compare_convert_fusion, s32[32]{0:T(128)S(1)} %bitcast.75), kind=kOutput, calls=%fused_computation.9 | convolution fusion | flops 63439168 | bytes 2752768 | tf_op jit(solution)/shard_map/ts,tbf->sbf/dot_general | solution.py:83
  86.4 1.0 pad_maximum_fusion
  87.8 0.5 collective-permute-start.3
  88.3 1.1 collective-permute-done.2
  89.4 2.1 %collective-permute-done.3 = bf16[32,512]{1,0:T(8,128)(2,1)S(1)} collective-permute-done((bf16[32,512]{1,0:T(8,128)(2,1)S(1)}, bf16[32,512]{1,0:T(8,128)(2,1)S(1)}, u32[]{:S(2)}, u32[]{:S(2)}) %collective-permute-start.3) | collective-permute-done | bytes 32800 | tf_op jit(solution)/shard_map/ppermute | solution.py:25
  91.5 60.2 %reduce-scatter.2.cloned.1.call-done = bf16[96,512]{1,0:T(8,128)(2,1)} async-done(((bf16[768,512]{1,0:T(8,128)(2,1)}), bf16[96,512]{1,0:T(8,128)(2,1)}) %reduce-scatter.2.cloned.1.call-update) | async-done | bytes 98320 | tf_op jit(solution)/shard_map/reduce_scatter | solution.py:95
  151.7 0.8 add_dynamic-update-slice_fusion
  152.5 1.0 convert_bitcast_fusion
  153.5 5.8 %all-gather.1 = bf16[256,512]{1,0:T(8,128)(2,1)S(1)} all-gather(bf16[64,512]{1,0:T(8,128)(2,1)S(1)} %slice-done), channel_id=3, replica_groups=mesh['dom'=8,'cluster'=4] {'cluster'}, dimensions={0}, use_global_device_ids=true | all-gather | bytes 327680 | tf_op jit(solution)/shard_map/all_gather | solution.py:100
  159.3 0.7 convert_element_type.92
  (33 shorter events, 1.8 us)
Async XLA Ops:
  7.2 66.6 %copy-start = (bf16[512,512]{1,0:T(8,128)(2,1)S(1)}, bf16[512,512]{1,0:T(8,128)(2,1)}, u32[]{:S(2)}) copy-start(bf16[512,512]{1,0:T(8,128)(2,1)} %param.18) | copy-start | bytes 1572868
  7.2 42.2 %copy-start.1 = (bf16[1,32,32,128]{3,2,1,0:T(8,128)(2,1)S(1)}, bf16[1,32,32,128]{3,2,1,0:T(8,128)(2,1)}, u32[]{:S(2)}) copy-start(bf16[1,32,32,128]{3,2,1,0:T(8,128)(2,1)} %param.14) | copy-start | bytes 786436
  7.2 144.5 %reduce-scatter.2.cloned.1.call-start = ((), (), s32[]{:S(2)}) async-start(), calls=%async_computation.1 | async-start | bytes 884736 | tf_op jit(solution)/shard_map/reduce_scatter | solution.py:95
  8.7 40.0 %collective-permute-start = (bf16[1,32,512]{2,1,0:T(8,128)(2,1)S(1)}, bf16[1,32,512]{2,1,0:T(8,128)(2,1)S(1)}, u32[]{:S(2)}, u32[]{:S(2)}) collective-permute-start(bf16[1,32,512]{2,1,0:T(8,128)(2,1)S(1)} %constant_dynamic-slice_fusion), channel_id=1, source_target_pairs={{0,1},{1,2},{2,3},{3,0},{4,5},{5,6},{6,7},{7,4},{8,9},{9,10},{10,1... | collective-permute-start | bytes 98312 | tf_op jit(solution)/shard_map/ppermute | solution.py:14
  9.2 39.5 %collective-permute-start.1 = (bf16[1,32,512]{2,1,0:T(8,128)(2,1)S(1)}, bf16[1,32,512]{2,1,0:T(8,128)(2,1)S(1)}, u32[]{:S(2)}, u32[]{:S(2)}) collective-permute-start(bf16[1,32,512]{2,1,0:T(8,128)(2,1)S(1)} %constant_dynamic-slice_fusion), channel_id=1, source_target_pairs={{1,0},{2,1},{3,2},{0,3},{5,4},{6,5},{7,6},{4,7},{9,8},{10,9},{11,1... | collective-permute-start | bytes 98312 | tf_op jit(solution)/shard_map/ppermute | solution.py:16
  54.1 10.3 %copy-start.5 = (s32[1,32]{1,0:T(1,128)S(1)}, s32[1,32]{1,0:T(1,128)}, u32[]{:S(2)}) copy-start(s32[1,32]{1,0:T(1,128)} %param.15) | copy-start | bytes 388
  71.1 1.1 copy-start.2
  72.3 1.5 copy-start.7
  75.7 1.1 copy-start.3
  81.0 3.1 %copy-start.6 = (s32[1,32]{1,0:T(1,128)S(1)}, s32[1,32]{1,0:T(1,128)}, u32[]{:S(2)}) copy-start(s32[1,32]{1,0:T(1,128)} %param.16) | copy-start | bytes 388
  84.1 2.2 %copy-start.4 = (bf16[8,64,512]{2,1,0:T(8,128)(2,1)S(1)}, bf16[8,64,512]{2,1,0:T(8,128)(2,1)}, u32[]{:S(2)}) copy-start(bf16[8,64,512]{2,1,0:T(8,128)(2,1)} %convolution_convert_fusion.1) | copy-start | bytes 1572868
  87.7 1.7 collective-permute-start.2
  87.8 3.7 %collective-permute-start.3 = (bf16[32,512]{1,0:T(8,128)(2,1)S(1)}, bf16[32,512]{1,0:T(8,128)(2,1)S(1)}, u32[]{:S(2)}, u32[]{:S(2)}) collective-permute-start(bf16[32,512]{1,0:T(8,128)(2,1)S(1)} %get-tuple-element.6), channel_id=1, source_target_pairs={{0,1},{1,2},{2,3},{3,0},{4,5},{5,6},{6,7},{7,4},{8,9},{9,10},{10,1... | collective-permute-start | bytes 98312 | tf_op jit(solution)/shard_map/ppermute | solution.py:25
  151.7 1.8 %slice-start = ((bf16[96,512]{1,0:T(8,128)(2,1)}), bf16[64,512]{1,0:T(8,128)(2,1)S(1)}, s32[]{:S(2)}) async-start(bf16[96,512]{1,0:T(8,128)(2,1)} %reduce-scatter.2.cloned.1.call-done), calls=%async_computation.2 | async-start | bytes 131072 | tf_op jit(solution)/shard_map/slice | solution.py:100
Sparse Core Ops, SparseCore 0:
  87.5 64.1 reduce-scatter.1
